TPU v7x, 32 devices: a whole 2x2x4 slice. The times are simulated.
32 devices in a mesh: slides: 2 (over y), seq: 4 (over z), head: 4 (over x, core).
Axes of the slice: x: 2, y: 2, z: 4, core: 2. Of those that a mesh axis runs over, the one named last changes fastest.
Arguments:
- query_rows: bfloat16 [8192, 768], P(('slides', 'seq'), 'head'), parts along dimension 0, may hold values from -64 to 64
- key_rows: bfloat16 [8192, 768], P(('slides', 'seq'), 'head'), parts along dimension 0, may hold values from -4.1 to 4.1
- value_rows: bfloat16 [8192, 768], P(('slides', 'seq'), 'head'), parts along dimension 0, may hold values from -6 to 6
Outputs:
- attended: bfloat16 [8192, 768], P(('slides', 'seq'), 'head'), parts along dimension 0
There are 2 independent parts, one for each index of `slides`. A program takes and returns all parts, laid end to end along the dimension named above; each array names one. Nothing has to cross between parts.
All inputs are finite; a program needn't handle non-finite values.
Results may differ from a plain program's by a relative error of at most 0.0028.
Values may be sent and summed in bfloat16 or wider, within the bound.
No kernel may reach another device: no remote copies, remote signals or barrier semaphores. Data moves between devices by JAX's collectives and lax.ppermute only.
A program may use at most 64 MiB of HBM per device.

v0:
```python
import math
import jax
import jax.numpy as jnp
import numpy as np
from jax import lax
from jax.sharding import PartitionSpec as P

HEAD_DIM = 48
SEG_A = 1024
SEG_B = 4096


def swapped(shard, axis, stride):
    return lax.ppermute(shard, axis, [(i, i ^ 1 << stride) for i in range(lax.axis_size(axis))])


def attend(query_flat, key_flat, value_flat, score_scale):
    local_heads = query_flat.shape[1] // HEAD_DIM
    query_block = query_flat.reshape(query_flat.shape[0], local_heads, HEAD_DIM)
    key_block = key_flat.reshape(key_flat.shape[0], local_heads, HEAD_DIM)
    value_block = value_flat.reshape(value_flat.shape[0], local_heads, HEAD_DIM)
    scores = (
        jnp.einsum("qad,kad->qak", query_block, key_block, preferred_element_type=jnp.float32)
        * score_scale
    )
    row_max = jnp.max(scores, axis=-1)
    exp_scores = jnp.exp(scores - row_max[:, :, None])
    row_total = jnp.sum(exp_scores, axis=-1)
    weighted = jnp.einsum(
        "qak,kad->qad",
        exp_scores.astype(jnp.bfloat16),
        value_block,
        preferred_element_type=jnp.float32,
    )
    level_out = weighted / row_total[:, :, None]
    return (
        level_out.reshape(query_flat.shape[0], local_heads * HEAD_DIM),
        row_max + jnp.log(row_total),
    )


def attend_rows(query_flat, key_flat, value_flat, score_scale):
    count, feature_width = query_flat.shape
    local_heads = feature_width // HEAD_DIM
    keys = key_flat.shape[0]
    rows = math.gcd(count, max(1, 1048576 // (local_heads * keys)))

    def one_piece(query_piece):
        return attend(query_piece, key_flat, value_flat, score_scale)

    outs, lses = lax.map(one_piece, query_flat.reshape(count // rows, rows, feature_width))
    return (outs.reshape(count, feature_width), lses.reshape(count, local_heads))


def local_segments(query_flat, key_flat, value_flat, seg_rows, score_scale):
    count, feature_width = query_flat.shape
    local_heads = feature_width // HEAD_DIM
    shape = (count // seg_rows, seg_rows, feature_width)

    def one_segment(parts):
        return attend_rows(parts[0], parts[1], parts[2], score_scale)

    outs, lses = lax.map(
        one_segment, (query_flat.reshape(shape), key_flat.reshape(shape), value_flat.reshape(shape))
    )
    return (outs.reshape(count, feature_width), lses.reshape(count, local_heads))


def pick_rows(block, stride):
    row_count, feature_width = block.shape
    local_heads = feature_width // HEAD_DIM
    grid = block.reshape(row_count // stride, stride * feature_width)
    columns = []
    for head in range(local_heads):
        begin = head % stride * feature_width + head * HEAD_DIM
        columns.append(grid[:, begin : begin + HEAD_DIM])
    return jnp.concatenate(columns, axis=1)


def spread_rows(level_out, level_lse, stride):
    used_count, feature_width = level_out.shape
    local_heads = feature_width // HEAD_DIM
    head_of_column = np.arange(feature_width) // HEAD_DIM
    out_phases = []
    lse_phases = []
    for phase in range(stride):
        column_mask = jnp.asarray((head_of_column % stride == phase).astype(np.float32))
        head_mask = jnp.asarray(np.arange(local_heads) % stride == phase)
        out_phases.append(level_out * column_mask[None, :])
        lse_phases.append(jnp.where(head_mask[None, :], level_lse, -jnp.inf))
    full_out = jnp.stack(out_phases, axis=1).reshape(used_count * stride, feature_width)
    full_lse = jnp.stack(lse_phases, axis=1).reshape(used_count * stride, local_heads)
    return (full_out, full_lse)


def fold_block(fold_state, queries, keys, values, valid, score_scale):
    running_max, running_total, running_acc = fold_state
    local_heads = queries.shape[1] // HEAD_DIM
    query_block = queries.reshape(queries.shape[0], local_heads, HEAD_DIM)
    key_block = keys.reshape(keys.shape[0], local_heads, HEAD_DIM)
    value_block = values.reshape(values.shape[0], local_heads, HEAD_DIM)
    scores = (
        jnp.einsum("qad,kad->qak", query_block, key_block, preferred_element_type=jnp.float32)
        * score_scale
    )
    scores = jnp.where(valid[None, None, :], scores, -jnp.inf)
    new_max = jnp.maximum(running_max, jnp.max(scores, axis=-1))
    safe_max = jnp.where(new_max == -jnp.inf, 0.0, new_max)
    rescale = jnp.exp(running_max - safe_max)
    exp_scores = jnp.exp(scores - safe_max[:, :, None])
    new_total = running_total * rescale + jnp.sum(exp_scores, axis=-1)
    weighted = jnp.einsum(
        "qak,kad->qad",
        exp_scores.astype(jnp.bfloat16),
        value_block,
        preferred_element_type=jnp.float32,
    )
    new_acc = running_acc * rescale[:, :, None] + weighted
    return (new_max, new_total, new_acc)


def per_device(query_rows, key_rows, value_rows):
    row_count = query_rows.shape[0]
    feature_width = query_rows.shape[1]
    local_heads = feature_width // HEAD_DIM
    shards = lax.axis_size("seq")
    score_scale = HEAD_DIM ** (-0.5)
    first_out, first_lse = local_segments(query_rows, key_rows, value_rows, SEG_A, score_scale)
    used_two = row_count // 2
    seg_two = SEG_B // 2
    query_two = pick_rows(query_rows, 2)
    key_two = pick_rows(key_rows, 2)
    value_two = pick_rows(value_rows, 2)
    stacked = jnp.stack([key_two, value_two])
    for bit_index in range((seg_two // used_two).bit_length() - 1):
        partner = swapped(stacked, "seq", bit_index)
        stacked = jnp.concatenate([stacked, partner], axis=1)
    second_out, second_lse = attend_rows(query_two, stacked[0], stacked[1], score_scale)
    span_tokens = row_count * shards
    group_span = span_tokens // row_count
    used_three = row_count // 4
    wide_queries = pick_rows(query_rows, 4)
    wide_keys = pick_rows(key_rows, 4)
    wide_values = pick_rows(value_rows, 4)
    my_group = lax.axis_index("seq") // group_span
    key_limit = max(1, 1048576 // (local_heads * used_three))
    initial = (
        jnp.full((used_three, local_heads), -jnp.inf, jnp.float32),
        jnp.zeros((used_three, local_heads), jnp.float32),
        jnp.zeros((used_three, local_heads, HEAD_DIM), jnp.float32),
    )
    pieces = (
        lax.all_gather(wide_keys, "seq", axis=0, tiled=True),
        lax.all_gather(wide_values, "seq", axis=0, tiled=True),
    )
    piece_rows = pieces[0].shape[0]
    block = math.gcd(piece_rows, key_limit)
    key_blocks = pieces[0].reshape(piece_rows // block, block, feature_width)
    value_blocks = pieces[1].reshape(piece_rows // block, block, feature_width)
    block_starts = jnp.arange(piece_rows // block, dtype=jnp.int32) * block

    def fold_step(inner_state, items):
        owners = (items[2] + jnp.arange(block, dtype=jnp.int32)) // used_three
        valid = owners // group_span == my_group
        return (fold_block(inner_state, wide_queries, items[0], items[1], valid, score_scale), None)

    final_state, unused = lax.scan(fold_step, initial, (key_blocks, value_blocks, block_starts))
    final_max, final_total, final_acc = final_state
    third_out = (final_acc / final_total[:, :, None]).reshape(used_three, feature_width)
    third_lse = final_max + jnp.log(final_total)
    second_full, second_lse_full = spread_rows(second_out, second_lse, 2)
    third_full, third_lse_full = spread_rows(third_out, third_lse, 4)
    peak = jnp.maximum(jnp.maximum(first_lse, second_lse_full), third_lse_full)
    weight_one = jnp.exp(first_lse - peak)
    weight_two = jnp.exp(second_lse_full - peak)
    weight_three = jnp.exp(third_lse_full - peak)
    denominator = jnp.repeat(weight_one + weight_two + weight_three, HEAD_DIM, axis=1)
    numerator = jnp.repeat(weight_one, HEAD_DIM, axis=1) * first_out
    numerator = numerator + jnp.repeat(weight_two, HEAD_DIM, axis=1) * second_full
    numerator = numerator + jnp.repeat(weight_three, HEAD_DIM, axis=1) * third_full
    return (numerator / denominator).astype(jnp.bfloat16)


def solution(mesh):
    return jax.shard_map(
        per_device,
        mesh=mesh,
        in_specs=(
            P(("slides", "seq"), "head"),
            P(("slides", "seq"), "head"),
            P(("slides", "seq"), "head"),
        ),
        out_specs=P(("slides", "seq"), "head"),
        check_vma=False,
    )
```

profile of v0, /device:TPU:0, one launch (start us, length us, event | category | flops | bytes accessed | tf_op | source)
XLA Modules:
  0.0 164.0 jit_solution(786289299190109567)
XLA Ops:
  4.0 3.1 %collective-permute-start = (bf16[2,512,192]{2,1,0:T(8,128)(2,1)S(1)}, bf16[2,512,192]{2,1,0:T(8,128)(2,1)S(1)}, u32[]{:S(2)}, u32[]{:S(2)}) collective-permute-start(bf16[2,512,192]{2,1,0:T(8,128)(2,1)S(1)} %pad_maximum_fusion.4), channel_id=1, source_target_pairs={{0,4},{4,0},{8,12},{12,8},{1,5},{5,1},{9,13},{13,9},{2,6},{6,2},{1... | collective-permute-start | bytes 1179656 | tf_op jit(solution)/shard_map/ppermute | solution.py:14
  7.1 1.3 reshape.582
  8.4 1.3 reshape.571
  9.9 1.3 reshape.573
  13.0 19.4 %all_gather.7 = bf16[1024,192]{1,0:T(8,128)(2,1)S(1)} all-gather(bf16[256,192]{1,0:T(8,128)(2,1)S(1)} %pad_maximum_fusion.8), channel_id=1, replica_groups=mesh['slides'=2,'seq'=4,'head'=4] {'seq'}, dimensions={0}, use_global_device_ids=true | all-gather | bytes 491520 | tf_op jit(solution)/shard_map/all_gather | solution.py:154
  33.7 14.8 %all_gather.6 = bf16[1024,192]{1,0:T(8,128)(2,1)S(1)} all-gather(bf16[256,192]{1,0:T(8,128)(2,1)S(1)} %pad_maximum_fusion.6), channel_id=1, replica_groups=mesh['slides'=2,'seq'=4,'head'=4] {'seq'}, dimensions={0}, use_global_device_ids=true | all-gather | bytes 491520 | tf_op jit(solution)/shard_map/all_gather | solution.py:153
  50.1 1.4 bitcast_reduce_fusion.2
  51.5 1.9 %copy-done = f32[4,1024,256]{2,1,0:T(8,128)} copy-done((f32[4,1024,256]{2,1,0:T(8,128)}, f32[4,1024,256]{2,1,0:T(8,128)S(1)}, u32[]{:S(2)}) %copy-start) | copy-done | bytes 4194328
  54.4 35.3 %while.23 = (s32[]{:T(128)}, f32[4,256,192]{1,0,2:T(4,128)}, f32[4,256,4]{1,2,0:T(4,128)}, bf16[4,256,192]{1,2,0:T(8,128)(2,1)S(1)}, bf16[1024,192]{0,1:T(8,128)...) while((s32[]{:T(128)}, f32[4,256,192]{1,0,2:T(4,128)}, f32[4,256,4]{1,2,0:T(4,128)}, ...), condition=%wide.region_3.0_spmd, body=%wide.region_0.3_spmd.sunk | while | flops 209763328 | bytes 16253061 | solution.py:51
  57.4 5.3 %dynamic_update_slice.29 = f32[4,256,192]{1,0,2:T(4,128)} dynamic-update-slice(f32[4,256,192]{1,0,2:T(4,128)} %get-tuple-element.357, f32[1,256,192]{1,0,2:T(1,128)S(1)} %copy.156, s32[]{:T(128)S(6)} %copy.173, s32[]{:T(128)} %constant.135.clone.1..sunk, s32[]{:T(128)} %constant.135.clone.1..sunk) | dynamic-update-slice | bytes 393220 | tf_op jit(solution)/shard_map/while/body/eval_jaxpr/while/body/jit(dynamic_update_index_in_dim)/dynamic_update_slice | solution.py:51
  66.2 5.3 %dynamic_update_slice.29 = f32[4,256,192]{1,0,2:T(4,128)} dynamic-update-slice(f32[4,256,192]{1,0,2:T(4,128)} %get-tuple-element.357, f32[1,256,192]{1,0,2:T(1,128)S(1)} %copy.156, s32[]{:T(128)S(6)} %copy.173, s32[]{:T(128)} %constant.135.clone.1..sunk, s32[]{:T(128)} %constant.135.clone.1..sunk) | dynamic-update-slice | bytes 393220 | tf_op jit(solution)/shard_map/while/body/eval_jaxpr/while/body/jit(dynamic_update_index_in_dim)/dynamic_update_slice | solution.py:51
  75.0 5.3 %dynamic_update_slice.29 = f32[4,256,192]{1,0,2:T(4,128)} dynamic-update-slice(f32[4,256,192]{1,0,2:T(4,128)} %get-tuple-element.357, f32[1,256,192]{1,0,2:T(1,128)S(1)} %copy.156, s32[]{:T(128)S(6)} %copy.173, s32[]{:T(128)} %constant.135.clone.1..sunk, s32[]{:T(128)} %constant.135.clone.1..sunk) | dynamic-update-slice | bytes 393220 | tf_op jit(solution)/shard_map/while/body/eval_jaxpr/while/body/jit(dynamic_update_index_in_dim)/dynamic_update_slice | solution.py:51
  83.9 5.3 %dynamic_update_slice.29 = f32[4,256,192]{1,0,2:T(4,128)} dynamic-update-slice(f32[4,256,192]{1,0,2:T(4,128)} %get-tuple-element.357, f32[1,256,192]{1,0,2:T(1,128)S(1)} %copy.156, s32[]{:T(128)S(6)} %copy.173, s32[]{:T(128)} %constant.135.clone.1..sunk, s32[]{:T(128)} %constant.135.clone.1..sunk) | dynamic-update-slice | bytes 393220 | tf_op jit(solution)/shard_map/while/body/eval_jaxpr/while/body/jit(dynamic_update_index_in_dim)/dynamic_update_slice | solution.py:51
  89.8 3.5 %fusion.38 = f32[256,4,48]{0,2,1:T(8,128)S(1)} fusion(bf16[1024,4,48]{0,2,1:T(8,128)(2,1)} %bitcast.201, f32[4,1024,256]{2,1,0:T(8,128)} %copy-done, f32[256,4]{0,1:T(4,128)S(1)} %compare_select_fusion, pred[1024]{0:T(1024)(128)(4,1)S(1)} %fusion.45, f32[256,4]{0,1:T(4,128)S(1)} %get-tuple-element.237, f32[256,4]{0,1:T(4,128)S(1)} %get-tuple-element.236), kind=kOutput, calls=%fused_computation.35 | convolution fusion | flops 104955904 | bytes 4797440 | tf_op jit(solution)/shard_map/while/body/eval_jaxpr/qak,kad->qad/dot_general | solution.py:112
  99.4 1.3 pad_maximum_fusion.5
  101.5 2.2 %copy.152 = f32[24,8,4,256]{3,1,2,0:T(8,128)} copy(f32[24,8,4,256]{3,2,1,0:T(4,128)} %bitcast.199) | data formatting | bytes 1572864
  104.6 23.1 %collective-permute-done.1 = bf16[2,1024,192]{1,2,0:T(8,128)(2,1)} collective-permute-done((bf16[2,1024,192]{1,2,0:T(8,128)(2,1)}, bf16[2,1024,192]{1,2,0:T(8,128)(2,1)}, u32[]{:S(2)}, u32[]{:S(2)}) %collective-permute-start.1) | collective-permute-done | bytes 786464 | tf_op jit(solution)/shard_map/ppermute | solution.py:14
  127.7 1.3 pad_maximum_fusion
  129.1 29.1 %while.24 = (s32[]{:T(128)}, f32[4,128,192]{1,0,2:T(4,128)}, f32[4,128,4]{1,2,0:T(4,128)S(1)}, bf16[4,128,192]{1,2,0:T(8,128)(2,1)}, bf16[1,2048,192]{1,2,0:T(8,...) while((s32[]{:T(128)}, f32[4,128,192]{1,0,2:T(4,128)}, ...), condition=%wide.region_7.8_spmd, body=%wide.region_4.7_spmd.sunk | while | flops 209739264 | bytes 14614633 | solution.py:51
  132.6 3.9 %dynamic_update_slice.31 = f32[4,128,192]{1,0,2:T(4,128)} dynamic-update-slice(f32[4,128,192]{1,0,2:T(4,128)} %get-tuple-element.333, f32[1,128,192]{1,0,2:T(1,128)S(1)} %bitcast.189, s32[]{:T(128)S(6)} %copy.164, s32[]{:T(128)} %constant.135.clone.1..sunk.1, s32[]{:T(128)} %constant.135.clone.1..sunk.1) | dynamic-update-slice | bytes 196612 | tf_op jit(solution)/shard_map/while/body/jit(dynamic_update_index_in_dim)/dynamic_update_slice | solution.py:51
  139.8 3.9 %dynamic_update_slice.31 = f32[4,128,192]{1,0,2:T(4,128)} dynamic-update-slice(f32[4,128,192]{1,0,2:T(4,128)} %get-tuple-element.333, f32[1,128,192]{1,0,2:T(1,128)S(1)} %bitcast.189, s32[]{:T(128)S(6)} %copy.164, s32[]{:T(128)} %constant.135.clone.1..sunk.1, s32[]{:T(128)} %constant.135.clone.1..sunk.1) | dynamic-update-slice | bytes 196612 | tf_op jit(solution)/shard_map/while/body/jit(dynamic_update_index_in_dim)/dynamic_update_slice | solution.py:51
  147.1 3.9 %dynamic_update_slice.31 = f32[4,128,192]{1,0,2:T(4,128)} dynamic-update-slice(f32[4,128,192]{1,0,2:T(4,128)} %get-tuple-element.333, f32[1,128,192]{1,0,2:T(1,128)S(1)} %bitcast.189, s32[]{:T(128)S(6)} %copy.164, s32[]{:T(128)} %constant.135.clone.1..sunk.1, s32[]{:T(128)} %constant.135.clone.1..sunk.1) | dynamic-update-slice | bytes 196612 | tf_op jit(solution)/shard_map/while/body/jit(dynamic_update_index_in_dim)/dynamic_update_slice | solution.py:51
  154.4 3.9 %dynamic_update_slice.31 = f32[4,128,192]{1,0,2:T(4,128)} dynamic-update-slice(f32[4,128,192]{1,0,2:T(4,128)} %get-tuple-element.333, f32[1,128,192]{1,0,2:T(1,128)S(1)} %bitcast.189, s32[]{:T(128)S(6)} %copy.164, s32[]{:T(128)} %constant.135.clone.1..sunk.1, s32[]{:T(128)} %constant.135.clone.1..sunk.1) | dynamic-update-slice | bytes 196612 | tf_op jit(solution)/shard_map/while/body/jit(dynamic_update_index_in_dim)/dynamic_update_slice | solution.py:51
  161.9 2.2 %fusion.41 = bf16[1024,192]{0,1:T(8,128)(2,1)} fusion(f32[1024,192]{0,1:T(8,128)S(1)} %copy.142, f32[1024,192]{0,1:T(8,128)S(1)} %copy.137, f32[1024,192]{0,1:T(8,128)} %bitcast.193, f32[1024,4]{0,1:T(4,128)S(1)} %get-tuple-element.189, f32[1024,4]{0,1:T(4,128)S(1)} %get-tuple-element.192, f32[1024,4]{0,1:T(4,128)S(1)} %get-tuple-element.190, ...), kind=kLoop, calls=%fused_computation.40 | loop fusion | flops 1376256 | bytes 2818048 | tf_op jit(solution)/shard_map/convert_element_type | solution.py:181
  (145 shorter events, 49.0 us)
Async XLA Ops:
  2.4 7.2 %copy-start.2 = (bf16[1024,192]{0,1:T(8,128)(2,1)S(1)}, bf16[1024,192]{0,1:T(8,128)(2,1)}, u32[]{:S(2)}) copy-start(bf16[1024,192]{0,1:T(8,128)(2,1)} %param.19) | copy-start | bytes 1179652
  4.0 91.0 %collective-permute-start = (bf16[2,512,192]{2,1,0:T(8,128)(2,1)S(1)}, bf16[2,512,192]{2,1,0:T(8,128)(2,1)S(1)}, u32[]{:S(2)}, u32[]{:S(2)}) collective-permute-start(bf16[2,512,192]{2,1,0:T(8,128)(2,1)S(1)} %pad_maximum_fusion.4), channel_id=1, source_target_pairs={{0,4},{4,0},{8,12},{12,8},{1,5},{5,1},{9,13},{13,9},{2,6},{6,2},{1... | collective-permute-start | bytes 1179656 | tf_op jit(solution)/shard_map/ppermute | solution.py:14
  9.9 23.6 %copy-start.4 = (bf16[256,768]{1,0:T(8,128)(2,1)S(1)}, bf16[256,768]{1,0:T(8,128)(2,1)}, u32[]{:S(2)}) copy-start(bf16[256,768]{1,0:T(8,128)(2,1)} %reshape.571) | copy-start | bytes 1179652
  50.1 4.3 %copy-start.3 = (bf16[1024,192]{0,1:T(8,128)(2,1)S(1)}, bf16[1024,192]{0,1:T(8,128)(2,1)}, u32[]{:S(2)}) copy-start(bf16[1024,192]{0,1:T(8,128)(2,1)} %param.19) | copy-start | bytes 1179652
  50.1 4.3 %copy-start.1 = (bf16[1024,192]{0,1:T(8,128)(2,1)S(1)}, bf16[1024,192]{0,1:T(8,128)(2,1)}, u32[]{:S(2)}) copy-start(bf16[1024,192]{0,1:T(8,128)(2,1)} %param.20) | copy-start | bytes 1179652
  51.5 1.9 %copy-start = (f32[4,1024,256]{2,1,0:T(8,128)}, f32[4,1024,256]{2,1,0:T(8,128)S(1)}, u32[]{:S(2)}) copy-start(f32[4,1024,256]{2,1,0:T(8,128)S(1)} %get-tuple-element.239) | copy-start | bytes 12582916
  54.5 1.8 %copy-start.5 = (bf16[1024,192]{0,1:T(8,128)(2,1)S(1)}, bf16[1024,192]{0,1:T(8,128)(2,1)}, u32[]{:S(2)}) copy-start(bf16[1024,192]{0,1:T(8,128)(2,1)} %get-tuple-element.369) | copy-start | bytes 1179652 | tf_op jit(solution)/shard_map/while/body/eval_jaxpr/while
  63.3 1.8 %copy-start.5 = (bf16[1024,192]{0,1:T(8,128)(2,1)S(1)}, bf16[1024,192]{0,1:T(8,128)(2,1)}, u32[]{:S(2)}) copy-start(bf16[1024,192]{0,1:T(8,128)(2,1)} %get-tuple-element.369) | copy-start | bytes 1179652 | tf_op jit(solution)/shard_map/while/body/eval_jaxpr/while
  72.1 1.8 %copy-start.5 = (bf16[1024,192]{0,1:T(8,128)(2,1)S(1)}, bf16[1024,192]{0,1:T(8,128)(2,1)}, u32[]{:S(2)}) copy-start(bf16[1024,192]{0,1:T(8,128)(2,1)} %get-tuple-element.369) | copy-start | bytes 1179652 | tf_op jit(solution)/shard_map/while/body/eval_jaxpr/while
  80.9 1.8 %copy-start.5 = (bf16[1024,192]{0,1:T(8,128)(2,1)S(1)}, bf16[1024,192]{0,1:T(8,128)(2,1)}, u32[]{:S(2)}) copy-start(bf16[1024,192]{0,1:T(8,128)(2,1)} %get-tuple-element.369) | copy-start | bytes 1179652 | tf_op jit(solution)/shard_map/while/body/eval_jaxpr/while
  89.7 4.4 %copy-start.9 = (f32[192]{0:T(256)S(1)}, f32[192]{0:T(256)}, u32[]{:S(2)}) copy-start(f32[192]{0:T(256)} %constant.151.clone) | copy-start | bytes 2308
  89.7 4.4 %copy-start.10 = (f32[192]{0:T(256)S(1)}, f32[192]{0:T(256)}, u32[]{:S(2)}) copy-start(f32[192]{0:T(256)} %constant.153.clone) | copy-start | bytes 2308
  89.8 4.4 %copy-start.11 = (f32[192]{0:T(256)S(1)}, f32[192]{0:T(256)}, u32[]{:S(2)}) copy-start(f32[192]{0:T(256)} %constant.155.clone) | copy-start | bytes 2308
  89.8 4.4 %copy-start.12 = (f32[192]{0:T(256)S(1)}, f32[192]{0:T(256)}, u32[]{:S(2)}) copy-start(f32[192]{0:T(256)} %constant.157.clone) | copy-start | bytes 2308
  96.5 31.2 %collective-permute-start.1 = (bf16[2,1024,192]{1,2,0:T(8,128)(2,1)}, bf16[2,1024,192]{1,2,0:T(8,128)(2,1)}, u32[]{:S(2)}, u32[]{:S(2)}) collective-permute-start(bf16[2,1024,192]{1,2,0:T(8,128)(2,1)} %copy.122), channel_id=1, source_target_pairs={{0,8},{4,12},{8,0},{12,4},{1,9},{5,13},{9,1},{13,5},{2,10},{6,14},... | collective-permute-start | bytes 2359304 | tf_op jit(solution)/shard_map/ppermute | solution.py:14
  98.3 5.4 %copy-start.18 = (pred[4]{0:T(512)(128)(4,1)S(1)}, pred[4]{0:T(512)(128)(4,1)}, u32[]{:S(2)}) copy-start(pred[4]{0:T(512)(128)(4,1)} %constant.152.clone) | copy-start | bytes 16
  98.3 5.5 %copy-start.15 = (pred[4]{0:T(512)(128)(4,1)S(1)}, pred[4]{0:T(512)(128)(4,1)}, u32[]{:S(2)}) copy-start(pred[4]{0:T(512)(128)(4,1)} %constant.154.clone) | copy-start | bytes 16
  98.3 5.5 %copy-start.16 = (pred[4]{0:T(512)(128)(4,1)S(1)}, pred[4]{0:T(512)(128)(4,1)}, u32[]{:S(2)}) copy-start(pred[4]{0:T(512)(128)(4,1)} %constant.156.clone) | copy-start | bytes 16
  98.3 5.5 %copy-start.17 = (pred[4]{0:T(512)(128)(4,1)S(1)}, pred[4]{0:T(512)(128)(4,1)}, u32[]{:S(2)}) copy-start(pred[4]{0:T(512)(128)(4,1)} %constant.158.clone) | copy-start | bytes 16
  129.1 30.3 %copy-start.7 = (f32[192]{0:T(256)S(1)}, f32[192]{0:T(256)}, u32[]{:S(2)}) copy-start(f32[192]{0:T(256)} %constant.147.clone) | copy-start | bytes 2308
  129.1 30.3 %copy-start.8 = (f32[192]{0:T(256)S(1)}, f32[192]{0:T(256)}, u32[]{:S(2)}) copy-start(f32[192]{0:T(256)} %constant.149.clone) | copy-start | bytes 2308
  159.4 1.8 %copy-start.13 = (pred[4]{0:T(512)(128)(4,1)S(1)}, pred[4]{0:T(512)(128)(4,1)}, u32[]{:S(2)}) copy-start(pred[4]{0:T(512)(128)(4,1)} %constant.148.clone) | copy-start | bytes 16
  159.4 1.8 %copy-start.14 = (pred[4]{0:T(512)(128)(4,1)S(1)}, pred[4]{0:T(512)(128)(4,1)}, u32[]{:S(2)}) copy-start(pred[4]{0:T(512)(128)(4,1)} %constant.150.clone) | copy-start | bytes 16
  159.6 2.3 %copy-start.6 = (f32[4,256,4]{1,2,0:T(4,128)S(1)}, f32[4,256,4]{1,2,0:T(4,128)}, u32[]{:S(2)}) copy-start(f32[4,256,4]{1,2,0:T(4,128)} %get-tuple-element.113) | copy-start | bytes 49156
where the time goes:
time: 165 us; the launch traced here: 164 us
  local copies, waits for them, and re-layouts  64.5 us (39%)
  blocking collectives  34.2 us (21%)
  waiting for transfers between devices  23.1 us (14%)
  matrix products  18.9 us (11%)
  other arithmetic  18.8 us (11%)
  starting transfers between devices  3.83 us (2%)
    dynamic_update_slice x12, local copies, waits for them, and re-layouts, attend_rows(): lax.map(one_piece, query_flat.reshape(count // rows, rows, feature_width))  37.4 us
    ppermute x2, waiting for transfers between devices, swapped(): lax.ppermute(shard, axis, [(i, i ^ 1 << stride) for i in range(lax.axis_s...  23.1 us
    all_gather x1, blocking collectives, per_device(): lax.all_gather(wide_values, 'seq', axis=0, tiled=True)  19.4 us
    all_gather x1, blocking collectives, per_device(): lax.all_gather(wide_keys, 'seq', axis=0, tiled=True)  14.8 us
    dot_general x8, matrix products, attend(): jnp.einsum('qak,kad->qad', exp_scores.astype(jnp.bfloat16), value_block,...  7.47 us
    reduce_sum x8, other arithmetic, attend(): row_total = jnp.sum(exp_scores, axis=-1)  7.01 us
    unnamed x40, local copies, waits for them, and re-layouts  6.78 us
    dot_general x8, matrix products, attend(): jnp.einsum('qad,kad->qak', query_block, key_block, preferred_element_type...  6.63 us
  transfers between devices with their start and end apart: 2, of which 1 were waited for; matrix products, arithmetic and copies ran while one was open for 36% of the time, Pallas kernels for 0%

commit v1 on v0

--- a/solution.py
+++ b/solution.py
@@ -8,6 +8,27 @@
 HEAD_DIM = 48
 SEG_A = 1024
 SEG_B = 4096
+
+
+def collect(x, axis, dim):
+    size, index, rows = (lax.axis_size(axis), lax.axis_index(axis), x.shape[dim])
+    right = [(i, (i + 1) % size) for i in range(size)]
+    left = [(i, (i - 1) % size) for i in range(size)]
+    result = jnp.zeros((*x.shape[:dim], size * rows, *x.shape[dim + 1 :]), x.dtype)
+    result = lax.dynamic_update_slice_in_dim(result, x, index * rows, axis=dim)
+    from_left = from_right = x
+    halfway = size // 2
+    for step in range(1, halfway + 1):
+        from_left = lax.ppermute(from_left, axis, right)
+        result = lax.dynamic_update_slice_in_dim(
+            result, from_left, (index - step) % size * rows, axis=dim
+        )
+        if step < size - halfway:
+            from_right = lax.ppermute(from_right, axis, left)
+            result = lax.dynamic_update_slice_in_dim(
+                result, from_right, (index + step) % size * rows, axis=dim
+            )
+    return result
 
 
 def swapped(shard, axis, stride):
@@ -149,10 +170,7 @@
         jnp.zeros((used_three, local_heads), jnp.float32),
         jnp.zeros((used_three, local_heads, HEAD_DIM), jnp.float32),
     )
-    pieces = (
-        lax.all_gather(wide_keys, "seq", axis=0, tiled=True),
-        lax.all_gather(wide_values, "seq", axis=0, tiled=True),
-    )
+    pieces = (lax.all_gather(wide_keys, "seq", axis=0, tiled=True), collect(wide_values, "seq", 0))
     piece_rows = pieces[0].shape[0]
     block = math.gcd(piece_rows, key_limit)
     key_blocks = pieces[0].reshape(piece_rows // block, block, feature_width)

time: 165 us -> 158 us (0.958)
  blocking collectives: 34.2 us -> 22.7 us
  waiting for transfers between devices: 23.1 us -> 32.2 us
  local copies, waits for them, and re-layouts: 64.5 us -> 60.2 us
  other arithmetic: 18.8 us -> 16 us
  starting transfers between devices: 3.83 us -> 5.73 us
    all_gather x1 -> x0, blocking collectives: 19.4 us -> none  [per_device(): lax.all_gather(wide_values, 'seq', axis=0, tiled=True)]
    all_gather x1, blocking collectives: 14.8 us -> 22.7 us  [per_device(): lax.all_gather(wide_keys, 'seq', axis=0, tiled=True)]
    ppermute x0 -> x3, waiting for transfers between devices: none -> 6.48 us  [the longest x2 6.48 us: collect(): from_left = lax.ppermute(from_left, axis, right)]
    ppermute x0 -> x3, starting transfers between devices: none -> 5.66 us  [the longest x2 3.56 us: collect(): from_left = lax.ppermute(from_left, axis, right)]
    ppermute x2, starting transfers between devices: 3.83 us -> 0.07 us  [swapped(): lax.ppermute(shard, axis, [(i, i ^ 1 << stride) for i in range(lax.axis_s...]
    dynamic_slice x8, local copies, waits for them, and re-layouts: 3.26 us -> 0.06 us  [attend_rows(): lax.map(one_piece, query_flat.reshape(count // rows, rows, feature_width))]
    ppermute x2, waiting for transfers between devices: 23.1 us -> 25.8 us  [swapped(): lax.ppermute(shard, axis, [(i, i ^ 1 << stride) for i in range(lax.axis_s...]
    ppermute x0 -> x3, local copies, waits for them, and re-layouts: none -> 2.1 us  [the longest x2 1.1 us: collect(): from_left = lax.ppermute(from_left, axis, right)]
  transfers between devices with their start and end apart: 2 -> 5, of which waited for: 1 -> 2; matrix products, arithmetic and copies ran while one was open for 36% -> 36% of each run, Pallas kernels for 0% -> 0%
where the time goes in v1:
time: 158 us; the launch traced here: 157 us
  local copies, waits for them, and re-layouts  60.2 us (38%)
  waiting for transfers between devices  32.2 us (20%)
  blocking collectives  22.7 us (14%)
  matrix products  18.7 us (12%)
  other arithmetic  16 us (10%)
  starting transfers between devices  5.73 us (4%)
    dynamic_update_slice x12, local copies, waits for them, and re-layouts, attend_rows(): lax.map(one_piece, query_flat.reshape(count // rows, rows, feature_width))  37.6 us
    ppermute x2, waiting for transfers between devices, swapped(): lax.ppermute(shard, axis, [(i, i ^ 1 << stride) for i in range(lax.axis_s...  25.8 us
    all_gather x1, blocking collectives, per_device(): lax.all_gather(wide_keys, 'seq', axis=0, tiled=True)  22.7 us
    dot_general x8, matrix products, attend(): jnp.einsum('qak,kad->qad', exp_scores.astype(jnp.bfloat16), value_block,...  7.47 us
    reduce_sum x8, other arithmetic, attend(): row_total = jnp.sum(exp_scores, axis=-1)  7.01 us
    unnamed x40, local copies, waits for them, and re-layouts  6.78 us
    dot_general x8, matrix products, attend(): jnp.einsum('qad,kad->qak', query_block, key_block, preferred_element_type...  6.65 us
    ppermute x2, waiting for transfers between devices, collect(): from_left = lax.ppermute(from_left, axis, right)  6.48 us
  transfers between devices with their start and end apart: 5, of which 2 were waited for; matrix products, arithmetic and copies ran while one was open for 36% of the time, Pallas kernels for 0%

profile of v1, /device:TPU:0, one launch (start us, length us, event | category | flops | bytes accessed | tf_op | source)
XLA Modules:
  0.0 156.6 jit_solution(12595411561614695174)
XLA Ops:
  2.0 3.1 %collective-permute-start.2 = (bf16[256,192]{1,0:T(8,128)(2,1)S(1)}, bf16[256,192]{1,0:T(8,128)(2,1)}, u32[]{:S(2)}, u32[]{:S(2)}) collective-permute-start(bf16[256,192]{1,0:T(8,128)(2,1)S(1)} %pad_maximum_fusion.8), channel_id=1, source_target_pairs={{0,4},{4,8},{8,12},{12,0},{1,5},{5,9},{9,13},{13,1},{2,6},{6,10},{... | collective-permute-start | bytes 294920 | tf_op jit(solution)/shard_map/ppermute | solution.py:22
  5.1 2.1 %collective-permute-start.3 = (bf16[256,192]{1,0:T(8,128)(2,1)S(1)}, bf16[256,192]{1,0:T(8,128)(2,1)}, u32[]{:S(2)}, u32[]{:S(2)}) collective-permute-start(bf16[256,192]{1,0:T(8,128)(2,1)S(1)} %pad_maximum_fusion.8), channel_id=1, source_target_pairs={{0,12},{4,0},{8,4},{12,8},{1,13},{5,1},{9,5},{13,9},{2,14},{6,2},{... | collective-permute-start | bytes 294920 | tf_op jit(solution)/shard_map/ppermute | solution.py:27
  7.5 1.2 copy.129
  10.8 1.3 reshape.590
  12.8 22.7 %all_gather.3 = bf16[1024,192]{1,0:T(8,128)(2,1)S(1)} all-gather(bf16[256,192]{1,0:T(8,128)(2,1)S(1)} %pad_maximum_fusion.6), channel_id=1, replica_groups=mesh['slides'=2,'seq'=4,'head'=4] {'seq'}, dimensions={0}, use_global_device_ids=true | all-gather | bytes 491520 | tf_op jit(solution)/shard_map/all_gather | solution.py:173
  37.1 1.2 bitcast_reduce_fusion.2
  38.4 1.9 %copy-done = f32[4,1024,256]{2,1,0:T(8,128)} copy-done((f32[4,1024,256]{2,1,0:T(8,128)}, f32[4,1024,256]{2,1,0:T(8,128)S(1)}, u32[]{:S(2)}) %copy-start) | copy-done | bytes 4194328
  42.2 35.5 %while.23 = (s32[]{:T(128)}, f32[4,256,192]{1,0,2:T(4,128)}, f32[4,256,4]{1,2,0:T(4,128)}, bf16[4,256,192]{1,2,0:T(8,128)(2,1)S(1)}, bf16[1024,192]{0,1:T(8,128)...) while((s32[]{:T(128)}, f32[4,256,192]{1,0,2:T(4,128)}, f32[4,256,4]{1,2,0:T(4,128)}, ...), condition=%wide.region_3.0_spmd, body=%wide.region_0.3_spmd.sunk | while | flops 209763328 | bytes 16253061 | solution.py:72
  45.1 5.3 %dynamic_update_slice.57 = f32[4,256,192]{1,0,2:T(4,128)} dynamic-update-slice(f32[4,256,192]{1,0,2:T(4,128)} %get-tuple-element.357, f32[1,256,192]{1,0,2:T(1,128)S(1)} %copy.168, s32[]{:T(128)S(6)} %copy.189, s32[]{:T(128)} %constant.167.clone.1..sunk, s32[]{:T(128)} %constant.167.clone.1..sunk) | dynamic-update-slice | bytes 393220 | tf_op jit(solution)/shard_map/while/body/eval_jaxpr/while/body/jit(dynamic_update_index_in_dim)/dynamic_update_slice | solution.py:72
  54.0 5.3 %dynamic_update_slice.57 = f32[4,256,192]{1,0,2:T(4,128)} dynamic-update-slice(f32[4,256,192]{1,0,2:T(4,128)} %get-tuple-element.357, f32[1,256,192]{1,0,2:T(1,128)S(1)} %copy.168, s32[]{:T(128)S(6)} %copy.189, s32[]{:T(128)} %constant.167.clone.1..sunk, s32[]{:T(128)} %constant.167.clone.1..sunk) | dynamic-update-slice | bytes 393220 | tf_op jit(solution)/shard_map/while/body/eval_jaxpr/while/body/jit(dynamic_update_index_in_dim)/dynamic_update_slice | solution.py:72
  62.8 5.3 %dynamic_update_slice.57 = f32[4,256,192]{1,0,2:T(4,128)} dynamic-update-slice(f32[4,256,192]{1,0,2:T(4,128)} %get-tuple-element.357, f32[1,256,192]{1,0,2:T(1,128)S(1)} %copy.168, s32[]{:T(128)S(6)} %copy.189, s32[]{:T(128)} %constant.167.clone.1..sunk, s32[]{:T(128)} %constant.167.clone.1..sunk) | dynamic-update-slice | bytes 393220 | tf_op jit(solution)/shard_map/while/body/eval_jaxpr/while/body/jit(dynamic_update_index_in_dim)/dynamic_update_slice | solution.py:72
  71.7 5.3 %dynamic_update_slice.57 = f32[4,256,192]{1,0,2:T(4,128)} dynamic-update-slice(f32[4,256,192]{1,0,2:T(4,128)} %get-tuple-element.357, f32[1,256,192]{1,0,2:T(1,128)S(1)} %copy.168, s32[]{:T(128)S(6)} %copy.189, s32[]{:T(128)} %constant.167.clone.1..sunk, s32[]{:T(128)} %constant.167.clone.1..sunk) | dynamic-update-slice | bytes 393220 | tf_op jit(solution)/shard_map/while/body/eval_jaxpr/while/body/jit(dynamic_update_index_in_dim)/dynamic_update_slice | solution.py:72
  78.6 2.2 %copy.164 = f32[24,8,4,256]{3,1,2,0:T(8,128)} copy(f32[24,8,4,256]{3,2,1,0:T(4,128)} %bitcast.38) | data formatting | bytes 1572864
  84.0 6.5 %collective-permute-done.4 = bf16[256,192]{1,0:T(8,128)(2,1)S(1)} collective-permute-done((bf16[256,192]{1,0:T(8,128)(2,1)}, bf16[256,192]{1,0:T(8,128)(2,1)S(1)}, u32[]{:S(2)}, u32[]{:S(2)}) %collective-permute-start.4) | collective-permute-done | bytes 98336 | tf_op jit(solution)/shard_map/ppermute | solution.py:22
  90.8 1.2 copy.131
  92.7 3.4 %fusion.38 = f32[256,4,48]{0,2,1:T(8,128)S(1)} fusion(bf16[1024,4,48]{0,2,1:T(8,128)(2,1)} %bitcast.200, f32[4,1024,256]{2,1,0:T(8,128)} %copy-done, f32[256,4]{0,1:T(4,128)S(1)} %compare_select_fusion, pred[1024]{0:T(1024)(128)(4,1)S(1)} %fusion.45, f32[256,4]{0,1:T(4,128)S(1)} %get-tuple-element.237, f32[256,4]{0,1:T(4,128)S(1)} %get-tuple-element.236), kind=kOutput, calls=%fused_computation.35 | convolution fusion | flops 104955904 | bytes 4797440 | tf_op jit(solution)/shard_map/while/body/eval_jaxpr/qak,kad->qad/dot_general | solution.py:133
  97.7 25.8 %collective-permute-done.1 = bf16[2,1024,192]{1,2,0:T(8,128)(2,1)} collective-permute-done((bf16[2,1024,192]{1,2,0:T(8,128)(2,1)}, bf16[2,1024,192]{1,2,0:T(8,128)(2,1)}, u32[]{:S(2)}, u32[]{:S(2)}) %collective-permute-start.1) | collective-permute-done | bytes 786464 | tf_op jit(solution)/shard_map/ppermute | solution.py:35
  123.4 1.3 pad_maximum_fusion
  124.9 26.0 %while.24 = (s32[]{:T(128)}, f32[4,128,192]{1,0,2:T(4,128)}, f32[4,128,4]{1,2,0:T(4,128)S(1)}, bf16[4,128,192]{1,2,0:T(8,128)(2,1)S(1)}, bf16[1,2048,192]{1,2,0:...) while((s32[]{:T(128)}, f32[4,128,192]{1,0,2:T(4,128)}, ...), condition=%wide.region_7.8_spmd, body=%wide.region_4.7_spmd.sunk | while | flops 209739264 | bytes 14614633 | solution.py:72
  127.5 3.9 %dynamic_update_slice.59 = f32[4,128,192]{1,0,2:T(4,128)} dynamic-update-slice(f32[4,128,192]{1,0,2:T(4,128)} %get-tuple-element.333, f32[1,128,192]{1,0,2:T(1,128)S(1)} %bitcast.189, s32[]{:T(128)S(6)} %copy.180, s32[]{:T(128)} %constant.167.clone.1..sunk.1, s32[]{:T(128)} %constant.167.clone.1..sunk.1) | dynamic-update-slice | bytes 196612 | tf_op jit(solution)/shard_map/while/body/jit(dynamic_update_index_in_dim)/dynamic_update_slice | solution.py:72
  134.0 3.9 %dynamic_update_slice.59 = f32[4,128,192]{1,0,2:T(4,128)} dynamic-update-slice(f32[4,128,192]{1,0,2:T(4,128)} %get-tuple-element.333, f32[1,128,192]{1,0,2:T(1,128)S(1)} %bitcast.189, s32[]{:T(128)S(6)} %copy.180, s32[]{:T(128)} %constant.167.clone.1..sunk.1, s32[]{:T(128)} %constant.167.clone.1..sunk.1) | dynamic-update-slice | bytes 196612 | tf_op jit(solution)/shard_map/while/body/jit(dynamic_update_index_in_dim)/dynamic_update_slice | solution.py:72
  140.5 3.9 %dynamic_update_slice.59 = f32[4,128,192]{1,0,2:T(4,128)} dynamic-update-slice(f32[4,128,192]{1,0,2:T(4,128)} %get-tuple-element.333, f32[1,128,192]{1,0,2:T(1,128)S(1)} %bitcast.189, s32[]{:T(128)S(6)} %copy.180, s32[]{:T(128)} %constant.167.clone.1..sunk.1, s32[]{:T(128)} %constant.167.clone.1..sunk.1) | dynamic-update-slice | bytes 196612 | tf_op jit(solution)/shard_map/while/body/jit(dynamic_update_index_in_dim)/dynamic_update_slice | solution.py:72
  147.0 3.9 %dynamic_update_slice.59 = f32[4,128,192]{1,0,2:T(4,128)} dynamic-update-slice(f32[4,128,192]{1,0,2:T(4,128)} %get-tuple-element.333, f32[1,128,192]{1,0,2:T(1,128)S(1)} %bitcast.189, s32[]{:T(128)S(6)} %copy.180, s32[]{:T(128)} %constant.167.clone.1..sunk.1, s32[]{:T(128)} %constant.167.clone.1..sunk.1) | dynamic-update-slice | bytes 196612 | tf_op jit(solution)/shard_map/while/body/jit(dynamic_update_index_in_dim)/dynamic_update_slice | solution.py:72
  154.5 2.2 %fusion.41 = bf16[1024,192]{0,1:T(8,128)(2,1)} fusion(f32[1024,192]{0,1:T(8,128)S(1)} %copy.154, f32[1024,192]{0,1:T(8,128)S(1)} %copy.146, f32[1024,192]{0,1:T(8,128)} %bitcast.193, f32[1024,4]{0,1:T(4,128)S(1)} %get-tuple-element.189, f32[1024,4]{0,1:T(4,128)S(1)} %get-tuple-element.192, f32[1024,4]{0,1:T(4,128)S(1)} %get-tuple-element.190, ...), kind=kLoop, calls=%fused_computation.40 | loop fusion | flops 1376256 | bytes 2818048 | tf_op jit(solution)/shard_map/convert_element_type | solution.py:199
  (158 shorter events, 42.9 us)
Async XLA Ops:
  2.0 8.6 %copy-start.2 = (bf16[1024,192]{0,1:T(8,128)(2,1)S(1)}, bf16[1024,192]{0,1:T(8,128)(2,1)}, u32[]{:S(2)}) copy-start(bf16[1024,192]{0,1:T(8,128)(2,1)} %param.19) | copy-start | bytes 1179652
  2.0 79.4 %collective-permute-start.2 = (bf16[256,192]{1,0:T(8,128)(2,1)S(1)}, bf16[256,192]{1,0:T(8,128)(2,1)}, u32[]{:S(2)}, u32[]{:S(2)}) collective-permute-start(bf16[256,192]{1,0:T(8,128)(2,1)S(1)} %pad_maximum_fusion.8), channel_id=1, source_target_pairs={{0,4},{4,8},{8,12},{12,0},{1,5},{5,9},{9,13},{13,1},{2,6},{6,10},{... | collective-permute-start | bytes 294920 | tf_op jit(solution)/shard_map/ppermute | solution.py:22
  5.1 77.8 %collective-permute-start.3 = (bf16[256,192]{1,0:T(8,128)(2,1)S(1)}, bf16[256,192]{1,0:T(8,128)(2,1)}, u32[]{:S(2)}, u32[]{:S(2)}) collective-permute-start(bf16[256,192]{1,0:T(8,128)(2,1)S(1)} %pad_maximum_fusion.8), channel_id=1, source_target_pairs={{0,12},{4,0},{8,4},{12,8},{1,13},{5,1},{9,5},{13,9},{2,14},{6,2},{... | collective-permute-start | bytes 294920 | tf_op jit(solution)/shard_map/ppermute | solution.py:27
  10.0 80.5 %collective-permute-start = (bf16[2,512,192]{2,1,0:T(8,128)(2,1)S(1)}, bf16[2,512,192]{2,1,0:T(8,128)(2,1)S(1)}, u32[]{:S(2)}, u32[]{:S(2)}) collective-permute-start(bf16[2,512,192]{2,1,0:T(8,128)(2,1)S(1)} %pad_maximum_fusion.4), channel_id=1, source_target_pairs={{0,4},{4,0},{8,12},{12,8},{1,5},{5,1},{9,13},{13,9},{2,6},{6,2},{1... | collective-permute-start | bytes 1179656 | tf_op jit(solution)/shard_map/ppermute | solution.py:35
  38.4 1.9 %copy-start = (f32[4,1024,256]{2,1,0:T(8,128)}, f32[4,1024,256]{2,1,0:T(8,128)S(1)}, u32[]{:S(2)}) copy-start(f32[4,1024,256]{2,1,0:T(8,128)S(1)} %get-tuple-element.239) | copy-start | bytes 12582916
  38.4 3.7 %copy-start.1 = (bf16[1024,192]{0,1:T(8,128)(2,1)S(1)}, bf16[1024,192]{0,1:T(8,128)(2,1)}, u32[]{:S(2)}) copy-start(bf16[1024,192]{0,1:T(8,128)(2,1)} %param.20) | copy-start | bytes 1179652
  42.1 35.5 %copy-start.18 = (pred[4]{0:T(512)(128)(4,1)S(1)}, pred[4]{0:T(512)(128)(4,1)}, u32[]{:S(2)}) copy-start(pred[4]{0:T(512)(128)(4,1)} %constant.189.clone) | copy-start | bytes 16
  42.1 35.6 %copy-start.3 = (bf16[512,48]{1,0:T(8,128)(2,1)S(1)}, bf16[512,48]{1,0:T(8,128)(2,1)}, u32[]{:S(2)}) copy-start(bf16[512,48]{1,0:T(8,128)(2,1)} %get-tuple-element.214) | copy-start | bytes 147460
  42.1 35.8 %copy-start.15 = (pred[4]{0:T(512)(128)(4,1)S(1)}, pred[4]{0:T(512)(128)(4,1)}, u32[]{:S(2)}) copy-start(pred[4]{0:T(512)(128)(4,1)} %constant.191.clone) | copy-start | bytes 16
  42.1 35.8 %copy-start.16 = (pred[4]{0:T(512)(128)(4,1)S(1)}, pred[4]{0:T(512)(128)(4,1)}, u32[]{:S(2)}) copy-start(pred[4]{0:T(512)(128)(4,1)} %constant.193.clone) | copy-start | bytes 16
  42.1 35.8 %copy-start.17 = (pred[4]{0:T(512)(128)(4,1)S(1)}, pred[4]{0:T(512)(128)(4,1)}, u32[]{:S(2)}) copy-start(pred[4]{0:T(512)(128)(4,1)} %constant.195.clone) | copy-start | bytes 16
  42.2 1.8 %copy-start.4 = (bf16[1024,192]{0,1:T(8,128)(2,1)S(1)}, bf16[1024,192]{0,1:T(8,128)(2,1)}, u32[]{:S(2)}) copy-start(bf16[1024,192]{0,1:T(8,128)(2,1)} %get-tuple-element.369) | copy-start | bytes 1179652 | tf_op jit(solution)/shard_map/while/body/eval_jaxpr/while
  82.4 8.0 %collective-permute-start.4 = (bf16[256,192]{1,0:T(8,128)(2,1)}, bf16[256,192]{1,0:T(8,128)(2,1)S(1)}, u32[]{:S(2)}, u32[]{:S(2)}) collective-permute-start(bf16[256,192]{1,0:T(8,128)(2,1)} %collective-permute-done.2), channel_id=1, source_target_pairs={{0,4},{4,8},{8,12},{12,0},{1,5},{5,9},{9,13},{13,1},{2,6},{6,10},{... | collective-permute-start | bytes 294920 | tf_op jit(solution)/shard_map/ppermute | solution.py:22
  84.0 6.6 %copy-start.5 = (bf16[1024,192]{0,1:T(8,128)(2,1)}, bf16[1024,192]{0,1:T(8,128)(2,1)S(1)}, u32[]{:S(2)}) copy-start(bf16[1024,192]{0,1:T(8,128)(2,1)S(1)} %constant_dynamic-update-slice_fusion.1) | copy-start | bytes 1179652
  90.8 5.4 %copy-start.9 = (f32[192]{0:T(256)S(1)}, f32[192]{0:T(256)}, u32[]{:S(2)}) copy-start(f32[192]{0:T(256)} %constant.188.clone) | copy-start | bytes 2308
  90.8 5.4 %copy-start.10 = (f32[192]{0:T(256)S(1)}, f32[192]{0:T(256)}, u32[]{:S(2)}) copy-start(f32[192]{0:T(256)} %constant.190.clone) | copy-start | bytes 2308
  90.8 5.4 %copy-start.11 = (f32[192]{0:T(256)S(1)}, f32[192]{0:T(256)}, u32[]{:S(2)}) copy-start(f32[192]{0:T(256)} %constant.192.clone) | copy-start | bytes 2308
  90.8 5.4 %copy-start.12 = (f32[192]{0:T(256)S(1)}, f32[192]{0:T(256)}, u32[]{:S(2)}) copy-start(f32[192]{0:T(256)} %constant.194.clone) | copy-start | bytes 2308
  92.0 31.4 %collective-permute-start.1 = (bf16[2,1024,192]{1,2,0:T(8,128)(2,1)}, bf16[2,1024,192]{1,2,0:T(8,128)(2,1)}, u32[]{:S(2)}, u32[]{:S(2)}) collective-permute-start(bf16[2,1024,192]{1,2,0:T(8,128)(2,1)} %copy.131), channel_id=1, source_target_pairs={{0,8},{4,12},{8,0},{12,4},{1,9},{5,13},{9,1},{13,5},{2,10},{6,14},... | collective-permute-start | bytes 2359304 | tf_op jit(solution)/shard_map/ppermute | solution.py:35
  124.8 27.2 %copy-start.7 = (f32[192]{0:T(256)S(1)}, f32[192]{0:T(256)}, u32[]{:S(2)}) copy-start(f32[192]{0:T(256)} %constant.184.clone) | copy-start | bytes 2308
  124.9 27.2 %copy-start.8 = (f32[192]{0:T(256)S(1)}, f32[192]{0:T(256)}, u32[]{:S(2)}) copy-start(f32[192]{0:T(256)} %constant.186.clone) | copy-start | bytes 2308
  152.0 1.8 %copy-start.13 = (pred[4]{0:T(512)(128)(4,1)S(1)}, pred[4]{0:T(512)(128)(4,1)}, u32[]{:S(2)}) copy-start(pred[4]{0:T(512)(128)(4,1)} %constant.185.clone) | copy-start | bytes 16
  152.0 1.8 %copy-start.14 = (pred[4]{0:T(512)(128)(4,1)S(1)}, pred[4]{0:T(512)(128)(4,1)}, u32[]{:S(2)}) copy-start(pred[4]{0:T(512)(128)(4,1)} %constant.187.clone) | copy-start | bytes 16
  152.2 2.3 %copy-start.6 = (f32[4,256,4]{1,2,0:T(4,128)S(1)}, f32[4,256,4]{1,2,0:T(4,128)}, u32[]{:S(2)}) copy-start(f32[4,256,4]{1,2,0:T(4,128)} %get-tuple-element.113) | copy-start | bytes 49156
  (3 other events, 5.3 us)
